TPU v7x, 128 devices: a whole 4x4x4 slice. The times are simulated.
128 devices in a mesh: tile: 32 (over x, z, core), dp: 4 (over y).
Axes of the slice: x: 4, y: 4, z: 4, core: 2. Of those that a mesh axis runs over, the one named last changes fastest.
Arguments:
- fields: bfloat16 [4, 64, 64, 64, 128], P('dp', 'tile'), may hold values from -6 to 6
- cotangent: bfloat16 [4, 64, 64, 64, 128], P('dp', 'tile'), may hold values from -6 to 6
- is_ocean: int32 [64], P('tile'), may hold values from 0 to 1, as said below
- neighbours: int32 [64, 8], P('tile'), may hold values from -1 to 63, as said below
- kernel: float32 [7, 7, 128], replicated, may hold values from -0.875 to 0.875
- conv_bias: float32 [128], replicated, may hold values from -3 to 3
- ln_gain: float32 [128], replicated, may hold values from 0.25 to 1.75
- ln_bias: float32 [128], replicated, may hold values from -3 to 3
- w_up: bfloat16 [128, 512], replicated, may hold values from -0.5 to 0.5
- up_bias: float32 [512], replicated, may hold values from -3 to 3
- w_down: bfloat16 [512, 128], replicated, may hold values from -0.25 to 0.25
- down_bias: float32 [128], replicated, may hold values from -3 to 3
- layer_scale: float32 [128], replicated, may hold values from 0.3 to 1
Outputs:
- grad_fields: bfloat16 [4, 64, 64, 64, 128], P('dp', 'tile')
- g_kernel: float32 [7, 7, 128], replicated
- g_conv_bias: float32 [128], replicated
- g_ln_gain: float32 [128], replicated
- g_ln_bias: float32 [128], replicated
- g_w_up: float32 [128, 512], replicated
- g_up_bias: float32 [512], replicated
- g_w_down: float32 [512, 128], replicated
- g_down_bias: float32 [128], replicated
- g_layer_scale: float32 [128], replicated
Inputs may be any that keep to these rules, and one draw needn't show every extreme that they name: `is_ocean`: slots follow a serpentine curve through the columns of a grid of 8 x 8 tiles, alternating direction from column to column; tiles of the first and last grid rows are ocean. Entry k of slot s names the slot of the tile adjacent in direction k (north, south, west, east, north-west, north-east, south-west, south-east), or -1 where that tile is land or outside the grid or slot s is land; the relation is symmetric; the north and south neighbours are slot s - 1 or s + 1, and every neighbour lies within 15 slots of s.
All inputs are finite; a program needn't handle non-finite values.
Results may differ from a plain program's by a relative error of at most 0.0071.
Values may be sent and summed in bfloat16 or wider, within the bound.
No kernel may reach another device: no remote copies, remote signals or barrier semaphores. Data moves between devices by JAX's collectives and lax.ppermute only.
A program may use at most 128 MiB of HBM per device.

v0:
```python
from functools import partial
import math

import jax
import jax.numpy as jnp
from jax import lax
from jax.sharding import PartitionSpec as P

TROWS = 8


EPSILON = 1e-06


def passed_along(value, axis, by):
    devices = lax.axis_size(axis)
    pairs = [(i, i + by) for i in range(devices) if 0 <= i + by < devices]
    return lax.ppermute(value, axis, pairs)


def rims_of(tile_block, rim_depth):
    extent = tile_block.shape[0]
    top_band = tile_block[:rim_depth]
    bottom = tile_block[extent - rim_depth :]
    left_band = jnp.transpose(tile_block[:, :rim_depth], (1, 0, 2))
    right_band = jnp.transpose(tile_block[:, extent - rim_depth :], (1, 0, 2))
    return jnp.stack([top_band, bottom, left_band, right_band], 0)


def assemble(own_tile, picked, valid_flags, first_layer, rim_depth):
    extent = own_tile.shape[0]

    def rim_piece(direction, which_strip):
        stripe = picked[direction][which_strip, first_layer : first_layer + rim_depth]
        return stripe * valid_flags[direction].astype(own_tile.dtype)

    north_rim = rim_piece(0, 1)
    south_rim = rim_piece(1, 0)
    west_rim = jnp.transpose(rim_piece(2, 1), (1, 0, 2))
    east_rim = jnp.transpose(rim_piece(3, 0), (1, 0, 2))
    north_west = jnp.transpose(rim_piece(4, 1)[:, extent - rim_depth :], (1, 0, 2))
    north_east = jnp.transpose(rim_piece(5, 0)[:, extent - rim_depth :], (1, 0, 2))
    south_west = jnp.transpose(rim_piece(6, 1)[:, :rim_depth], (1, 0, 2))
    south_east = jnp.transpose(rim_piece(7, 0)[:, :rim_depth], (1, 0, 2))
    top_band = jnp.concatenate([north_west, north_rim, north_east], 1)
    middle = jnp.concatenate([west_rim, own_tile, east_rim], 1)
    bottom = jnp.concatenate([south_west, south_rim, south_east], 1)
    return jnp.concatenate([top_band, middle, bottom], 0)


def depthwise(padded, kernel, extent):
    running_sum = jnp.zeros((extent, extent, padded.shape[2]), jnp.float32)
    for lag_row in range(7):
        for lag_col in range(7):
            window = padded[lag_row : lag_row + extent, lag_col : lag_col + extent].astype(
                jnp.float32
            )
            running_sum = running_sum + window * kernel[lag_row, lag_col]
    return running_sum


def transposed(grad_padded, kernel, extent):
    running_sum = jnp.zeros((extent, extent, grad_padded.shape[2]), jnp.float32)
    for lag_row in range(7):
        for lag_col in range(7):
            window = grad_padded[
                6 - lag_row : 6 - lag_row + extent, 6 - lag_col : 6 - lag_col + extent
            ].astype(jnp.float32)
            running_sum = running_sum + window * kernel[lag_row, lag_col]
    return running_sum


def kernel_terms(grad_tile, padded, extent):
    grad_values = grad_tile.astype(jnp.float32)
    stacked = []
    for lag_row in range(7):
        line_terms = []
        for lag_col in range(7):
            window = padded[lag_row : lag_row + extent, lag_col : lag_col + extent].astype(
                jnp.float32
            )
            line_terms.append(jnp.sum(grad_values * window, axis=(0, 1)))
        stacked.append(jnp.stack(line_terms, 0))
    return jnp.stack(stacked, 0)


def gelu_tanh(values):
    return jax.nn.gelu(values, approximate=True)


def contract_last(left_rows, right_matrix):
    return lax.dot_general(
        left_rows, right_matrix, (((1,), (1,)), ((), ())), preferred_element_type=jnp.float32
    )


def contract_first(left_rows, right_rows):
    return lax.dot_general(
        left_rows, right_rows, (((0,), (0,)), ((), ())), preferred_element_type=jnp.float32
    )


def layer_rows(
    conv_rows, cot_rows, ln_gain, ln_bias, w_up, up_bias, w_down, down_bias, layer_scale
):
    mean_value = jnp.mean(conv_rows, -1, keepdims=True)
    centred = conv_rows - mean_value
    variance = jnp.mean(centred * centred, -1, keepdims=True)
    inverse_scale = lax.rsqrt(variance + EPSILON)
    normed = centred * inverse_scale
    scaled = (normed * ln_gain + ln_bias).astype(jnp.bfloat16)
    hidden_sum = jnp.dot(scaled, w_up, preferred_element_type=jnp.float32) + up_bias
    activation = gelu_tanh(hidden_sum).astype(jnp.bfloat16)
    mixed = jnp.dot(activation, w_down, preferred_element_type=jnp.float32) + down_bias
    grad_mixed = (cot_rows * layer_scale).astype(jnp.bfloat16)
    grad_act = contract_last(grad_mixed, w_down)
    pullback = jax.vjp(gelu_tanh, hidden_sum)[1]
    grad_pre = pullback(grad_act)[0].astype(jnp.bfloat16)
    grad_scaled = contract_last(grad_pre, w_up)
    grad_normed = grad_scaled * ln_gain
    grad_conv = inverse_scale * (
        grad_normed
        - jnp.mean(grad_normed, -1, keepdims=True)
        - normed * jnp.mean(grad_normed * normed, -1, keepdims=True)
    )
    return (
        grad_conv.astype(jnp.bfloat16),
        mixed,
        grad_mixed,
        activation,
        grad_pre,
        scaled,
        grad_scaled,
        normed,
    )


def row_terms(
    cot_rows, mixed, grad_mixed, activation, grad_pre, scaled, grad_scaled, normed, grad_conv
):
    return (
        jnp.sum(grad_conv.astype(jnp.float32), 0),
        jnp.sum(grad_scaled * normed, 0),
        jnp.sum(grad_scaled, 0),
        contract_first(scaled, grad_pre),
        jnp.sum(grad_pre.astype(jnp.float32), 0),
        contract_first(activation, grad_mixed),
        jnp.sum(grad_mixed.astype(jnp.float32), 0),
        jnp.sum(cot_rows * mixed, 0),
    )


def local(
    fields,
    cotangent,
    is_ocean,
    neighbours,
    kernel,
    conv_bias,
    ln_gain,
    ln_bias,
    w_up,
    up_bias,
    w_down,
    down_bias,
    layer_scale,
):
    samples, slot_count, extent, channels = (
        fields.shape[0],
        fields.shape[1],
        fields.shape[2],
        fields.shape[4],
    )
    hidden_width = w_up.shape[1]
    tile_count = lax.axis_size("tile")
    reach_span = min((2 * TROWS + slot_count - 2) // slot_count, tile_count - 1)
    position = lax.axis_index("tile")
    vert_base = (position - 1) * slot_count
    side_base = (position - reach_span) * slot_count
    layer_params = (ln_gain, ln_bias, w_up, up_bias, w_down, down_bias, layer_scale)
    zero_terms = (
        jnp.zeros((7, 7, channels), jnp.float32),
        jnp.zeros((channels,), jnp.float32),
        jnp.zeros((channels,), jnp.float32),
        jnp.zeros((channels,), jnp.float32),
        jnp.zeros((channels, hidden_width), jnp.float32),
        jnp.zeros((hidden_width,), jnp.float32),
        jnp.zeros((hidden_width, channels), jnp.float32),
        jnp.zeros((channels,), jnp.float32),
        jnp.zeros((channels,), jnp.float32),
    )

    def collect(rim_set):
        adjacent = {}
        for offset in (1, -1):
            adjacent[offset] = passed_along(rim_set, "tile", offset)
        vertical = jnp.concatenate([adjacent[1], rim_set, adjacent[-1]], 1)
        distant = {}
        for distance in range(2, reach_span + 1):
            for offset in (distance, -distance):
                distant[offset] = passed_along(rim_set, "tile", offset)[:, :, 2:4]
        below_list = [distant[distance] for distance in range(reach_span, 1, -1)]
        above_list = [distant[-distance] for distance in range(2, reach_span + 1)]
        middle_list = [adjacent[1][:, :, 2:4], rim_set[:, :, 2:4], adjacent[-1][:, :, 2:4]]
        sideways = jnp.concatenate(below_list + middle_list + above_list, 1)
        bases = jnp.zeros((6,), jnp.int32) + side_base
        return (vertical, sideways, bases)

    def fetch_rims(vertical, sideways, bases, slot_ids):
        upright = jnp.clip(slot_ids[:2] - vert_base, 0, vertical.shape[0] - 1)
        lateral = jnp.clip(slot_ids[2:] - bases, 0, sideways.shape[0] - 1)
        picked = [vertical[upright[0]], vertical[upright[1]]]
        picked = picked + [sideways[lateral[slot_pick]] for slot_pick in range(6)]
        return (picked, slot_ids >= 0)

    grad_sums = zero_terms
    rims_x = jax.vmap(jax.vmap(partial(rims_of, rim_depth=3)))(fields)
    vertical_x, sideways_x, bases_x = collect(rims_x)
    sample = 0
    tile_stack = fields[sample]
    cot_stack = cotangent[sample]

    def first_work(slot_id):
        picked, valid_flags = fetch_rims(
            vertical_x[sample], sideways_x[sample], bases_x, neighbours[slot_id]
        )
        padded = assemble(tile_stack[slot_id], picked, valid_flags, 0, 3)
        conv_out = depthwise(padded, kernel, extent) + conv_bias
        cot_rows = cot_stack[slot_id].astype(jnp.float32).reshape(-1, channels)
        layer_parts = layer_rows(conv_out.reshape(-1, channels), cot_rows, *layer_params)
        grad_tile = layer_parts[0].reshape(extent, extent, channels)
        weight_terms = (kernel_terms(grad_tile, padded, extent),) + row_terms(
            cot_rows, *layer_parts[1:], layer_parts[0]
        )
        keep_flag = (is_ocean[slot_id] > 0).astype(jnp.float32)
        return (grad_tile, tuple((keep_flag * term for term in weight_terms)))

    def first_step(running, slot_id):
        grad_tile, weight_terms = first_work(slot_id)
        return (tuple((total + term for total, term in zip(running, weight_terms))), grad_tile)

    grad_sums, sample_grads = lax.scan(first_step, grad_sums, jnp.arange(slot_count))
    grad_tiles = [sample_grads]
    grad_stack = jnp.stack(grad_tiles, 0)
    rims_g = jax.vmap(jax.vmap(partial(rims_of, rim_depth=3)))(grad_stack)
    vertical_g, sideways_g, bases_g = collect(rims_g)
    sample = 0
    cot_stack = cotangent[sample]

    def second_step(slot_id):
        picked, valid_flags = fetch_rims(
            vertical_g[sample], sideways_g[sample], bases_g, neighbours[slot_id]
        )
        grad_padded = assemble(grad_stack[sample, slot_id], picked, valid_flags, 0, 3)
        result = cot_stack[slot_id].astype(jnp.float32) + transposed(grad_padded, kernel, extent)
        keep_flag = (is_ocean[slot_id] > 0).astype(jnp.float32)
        return (result * keep_flag).astype(jnp.bfloat16)

    outputs = [lax.map(second_step, jnp.arange(slot_count))]
    summed = lax.psum(
        (
            grad_sums[0],
            grad_sums[1],
            grad_sums[2],
            grad_sums[3],
            grad_sums[4],
            grad_sums[5],
            grad_sums[6],
            grad_sums[7],
            grad_sums[8],
        ),
        ("tile", "dp"),
    )
    grad_scale = 1.0 / math.sqrt(
        samples * lax.axis_size("dp") * slot_count * tile_count * extent * extent
    )
    return (
        jnp.stack(outputs, 0),
        summed[0] * grad_scale,
        summed[1] * grad_scale,
        summed[2] * grad_scale,
        summed[3] * grad_scale,
        summed[4] * grad_scale,
        summed[5] * grad_scale,
        summed[6] * grad_scale,
        summed[7] * grad_scale,
        summed[8] * grad_scale,
    )


def solution(mesh):
    placed = (
        P("dp", "tile", None, None, None),
        P("dp", "tile", None, None, None),
        P("tile"),
        P("tile", None),
        P(),
        P(),
        P(),
        P(),
        P(),
        P(),
        P(),
        P(),
        P(),
    )
    return jax.shard_map(
        local,
        mesh=mesh,
        in_specs=placed,
        out_specs=(P("dp", "tile", None, None, None), P(), P(), P(), P(), P(), P(), P(), P(), P()),
        check_vma=False,
    )
```

profile of v0, /device:TPU:1, one launch (start us, length us, event | category | flops | bytes accessed | tf_op | source)
XLA Modules:
  0.0 865.7 jit_solution(16494934024993436842)
XLA Ops:
  17.4 5.7 collective-permute-start.2
  25.1 5.1 collective-permute-start.4
  35.7 13.1 %collective-permute-done.2 = bf16[1,2,4,3,64,128]{5,4,3,2,1,0:T(8,128)(2,1)S(1)} collective-permute-done((bf16[1,2,4,3,64,128]{5,4,3,2,1,0:T(8,128)(2,1)S(1)}, bf16[1,2,4,3,64,128]{5,4,3,2,1,0:T(8,128)(2,1)S(1)}, u32[]{:S(2)}, u32[]{:S(2)}) %collective-permute-start.2) | collective-permute-done | bytes 393248 | tf_op jit(solution)/shard_map/ppermute | solution.py:18
  73.0 4.9 collective-permute-done.11
  77.9 10.7 %collective-permute-done.12 = bf16[1,2,4,3,64,128]{5,4,3,2,1,0:T(8,128)(2,1)S(1)} collective-permute-done((bf16[1,2,4,3,64,128]{5,4,3,2,1,0:T(8,128)(2,1)S(1)}, bf16[1,2,4,3,64,128]{5,4,3,2,1,0:T(8,128)(2,1)S(1)}, u32[]{:S(2)}, u32[]{:S(2)}) %collective-permute-start.12) | collective-permute-done | bytes 393248 | tf_op jit(solution)/shard_map/ppermute | solution.py:18
  88.6 8.4 collective-permute-done.13
  97.0 22.3 %collective-permute-done.14 = bf16[1,2,4,3,64,128]{5,4,3,2,1,0:T(8,128)(2,1)S(1)} collective-permute-done((bf16[1,2,4,3,64,128]{5,4,3,2,1,0:T(8,128)(2,1)S(1)}, bf16[1,2,4,3,64,128]{5,4,3,2,1,0:T(8,128)(2,1)S(1)}, u32[]{:S(2)}, u32[]{:S(2)}) %collective-permute-start.14) | collective-permute-done | bytes 393248 | tf_op jit(solution)/shard_map/ppermute | solution.py:18
  121.0 6.8 copy.25
  130.9 242.7 %while.43 = (s32[]{:T(128)}, f32[7,7,128]{2,1,0:T(8,128)}, f32[128]{0:T(128)}, f32[128]{0:T(128)}, f32[128]{0:T(128)}, /*index=5*/f32[128,512]{1,0:T(8,128)}, f3...) while((s32[]{:T(128)}, f32[7,7,128]{2,1,0:T(8,128)}, ...), condition=%wide.region_60.61_spmd.clone, body=%wide.region_0.60_spmd.clone.sunk | while | flops 3501007360 | bytes 273028160 | solution.py:242
  177.4 16.3 %fusion.232 = (f32[64,64]{1,0:T(8,128)S(1)}, f32[64,64,128]{2,1,0:T(8,128)S(1)}) fusion(f32[128]{0:T(128)S(1)} %get-tuple-element.1736, f32[128]{0:T(128)S(1)} %get-tuple-element.1527, bf16[67,70,128]{2,1,0:T(8,128)(2,1)S(1)} %get-tuple-element.1526, f32[128]{0:T(128)S(1)} %get-tuple-element.1528, f32[128]{0:T(128)S(1)} %get-tuple-element.1529, ...), kind=kLoop, calls=%fused_computation.494.clone.1 | loop fusion | flops 87027712 | bytes 47326208 | tf_op jit(solution)/shard_map/while/body/eval_jaxpr/reduce_sum | solution.py:106
  203.8 7.3 convert_reduce_fusion.6
  214.1 9.7 %fusion.234 = (f32[128]{0:T(128)}, f32[128]{0:T(128)}, f32[128]{0:T(128)}, f32[128]{0:T(128)}, f32[128]{0:T(128)}, /*index=5*/f32[128]{0:T(128)}, f32[128]{0:T(1...) fusion(bf16[67,70,128]{2,1,0:T(8,128)(2,1)S(1)} %get-tuple-elem, ...), kind=kLoop, calls=%fused_computation.301.clone.1 | loop fusion | flops 33027840 | bytes 24192512 | tf_op jit(solution)/shard_map/while/body/eval_jaxpr/reduce_sum | solution.py:82
  237.3 8.7 %fusion.235 = (f32[128]{0:T(128)}, f32[128]{0:T(128)}, f32[128]{0:T(128)}, f32[128]{0:T(128)}, f32[128]{0:T(128)}, /*index=5*/f32[128]{0:T(128)}, f32[128]{0:T(1...) fusion(bf16[67,70,128]{2,1,0:T(8,128)(2,1)S(1)} %get-tuple-element.1526, ...), kind=kLoop, calls=%fused_computation.283.clone.1 | loop fusion | flops 28834304 | bytes 8493056 | tf_op jit(solution)/shard_map/while/body/eval_jaxpr/reduce_sum | solution.py:82
  247.5 5.2 fusion.236
  291.5 16.3 %fusion.232 = (f32[64,64]{1,0:T(8,128)S(1)}, f32[64,64,128]{2,1,0:T(8,128)S(1)}) fusion(f32[128]{0:T(128)S(1)} %get-tuple-element.1736, f32[128]{0:T(128)S(1)} %get-tuple-element.1527, bf16[67,70,128]{2,1,0:T(8,128)(2,1)S(1)} %get-tuple-element.1526, f32[128]{0:T(128)S(1)} %get-tuple-element.1528, f32[128]{0:T(128)S(1)} %get-tuple-element.1529, ...), kind=kLoop, calls=%fused_computation.494.clone.1 | loop fusion | flops 87027712 | bytes 47326208 | tf_op jit(solution)/shard_map/while/body/eval_jaxpr/reduce_sum | solution.py:106
  317.8 7.3 convert_reduce_fusion.6
  328.1 9.7 %fusion.234 = (f32[128]{0:T(128)}, f32[128]{0:T(128)}, f32[128]{0:T(128)}, f32[128]{0:T(128)}, f32[128]{0:T(128)}, /*index=5*/f32[128]{0:T(128)}, f32[128]{0:T(1...) fusion(bf16[67,70,128]{2,1,0:T(8,128)(2,1)S(1)} %get-tuple-elem, ...), kind=kLoop, calls=%fused_computation.301.clone.1 | loop fusion | flops 33027840 | bytes 24192512 | tf_op jit(solution)/shard_map/while/body/eval_jaxpr/reduce_sum | solution.py:82
  351.3 8.7 %fusion.235 = (f32[128]{0:T(128)}, f32[128]{0:T(128)}, f32[128]{0:T(128)}, f32[128]{0:T(128)}, f32[128]{0:T(128)}, /*index=5*/f32[128]{0:T(128)}, f32[128]{0:T(1...) fusion(bf16[67,70,128]{2,1,0:T(8,128)(2,1)S(1)} %get-tuple-element.1526, ...), kind=kLoop, calls=%fused_computation.283.clone.1 | loop fusion | flops 28834304 | bytes 8493056 | tf_op jit(solution)/shard_map/while/body/eval_jaxpr/reduce_sum | solution.py:82
  361.5 5.2 fusion.236
  369.0 4.3 fusion.240
  376.5 6.5 collective-permute-start.23
  389.0 6.0 collective-permute-start.17
  396.4 82.6 %all-reduce = (f32[7,7,128]{2,1,0:T(8,128)S(1)}, f32[128]{0:T(128)S(1)}, f32[128]{0:T(128)S(1)}, f32[128]{0:T(128)S(1)}, f32[512]{0:T(512)S(1)}, /*index=5*/f32[128]{0:T(128)S(1)}, f32[128]{0:T(128)S(1)}) all-reduce(f32[7,7,128]{2,1,0:T(8,128)S(1)} %copy-done.21, ...), channel_id=1, replica_groups=mesh['tile'=32,'dp'=4] {'tile','dp'}, use_global_device_ids=true, to_apply=%region_63.64 | all-reduce | flops 7424 | bytes 59392 | tf_op jit(solution)/shard_map/psum | solution.py:260
  482.8 142.8 %all-reduce.4.cloned.1.call-done = (f32[128,512]{1,0:T(8,128)}, f32[512,128]{1,0:T(8,128)}) async-done(((f32[128,512]{1,0:T(8,128)}, f32[512,128]{1,0:T(8,128)}), (f32[128,512]{1,0:T(8,128)}, f32[512,128]{1,0:T(8,128)})) %all-reduce.4.cloned.1.call-update) | async-done | bytes 524304 | tf_op jit(solution)/shard_map/psum | solution.py:260
  636.9 6.0 collective-permute-start.21
  649.0 34.7 %collective-permute-done.19 = bf16[1,2,4,3,64,128]{5,3,4,1,0,2:T(4,128)(2,1)S(1)} collective-permute-done((bf16[1,2,4,3,64,128]{5,3,4,1,0,2:T(4,128)(2,1)S(1)}, bf16[1,2,4,3,64,128]{5,3,4,1,0,2:T(4,128)(2,1)S(1)}, u32[]{:S(2)}, u32[]{:S(2)}) %collective-permute-start.19) | collective-permute-done | bytes 393248 | tf_op jit(solution)/shard_map/ppermute | solution.py:18
  693.0 18.9 %collective-permute-done.26 = bf16[1,2,4,3,64,128]{5,3,4,1,0,2:T(4,128)(2,1)S(1)} collective-permute-done((bf16[1,2,4,3,64,128]{5,3,4,1,0,2:T(4,128)(2,1)S(1)}, bf16[1,2,4,3,64,128]{5,3,4,1,0,2:T(4,128)(2,1)S(1)}, u32[]{:S(2)}, u32[]{:S(2)}) %collective-permute-start.26) | collective-permute-done | bytes 393248 | tf_op jit(solution)/shard_map/ppermute | solution.py:18
  716.0 22.6 %collective-permute-done.30 = bf16[1,2,4,3,64,128]{5,3,4,1,0,2:T(4,128)(2,1)S(1)} collective-permute-done((bf16[1,2,4,3,64,128]{5,3,4,1,0,2:T(4,128)(2,1)S(1)}, bf16[1,2,4,3,64,128]{5,3,4,1,0,2:T(4,128)(2,1)S(1)}, u32[]{:S(2)}, u32[]{:S(2)}) %collective-permute-start.30) | collective-permute-done | bytes 393248 | tf_op jit(solution)/shard_map/ppermute | solution.py:18
  738.7 14.6 %collective-permute-done.31 = bf16[1,2,4,3,64,128]{5,3,4,1,0,2:T(4,128)(2,1)S(1)} collective-permute-done((bf16[1,2,4,3,64,128]{5,3,4,1,0,2:T(4,128)(2,1)S(1)}, bf16[1,2,4,3,64,128]{5,3,4,1,0,2:T(4,128)(2,1)S(1)}, u32[]{:S(2)}, u32[]{:S(2)}) %collective-permute-start.31) | collective-permute-done | bytes 393248 | tf_op jit(solution)/shard_map/ppermute | solution.py:18
  759.3 99.1 %while.42 = (s32[]{:T(128)}, bf16[2,64,64,128]{3,2,1,0:T(8,128)(2,1)}, s32[2]{0:T(128)S(1)}, bf16[2,64,64,128]{3,2,1,0:T(8,128)(2,1)S(1)}, s32[2,8]{1,0:T(2,128)...) while((s32[]{:T(128)}, ...), condition=%wide.region_62.63_spmd.clone, body=%wide.region_61.62_spmd.clone.sunk | while | flops 102684736 | bytes 53919052 | solution.py:259
  792.3 16.7 %bitcast_dynamic-update-slice_fusion.2 = bf16[2,64,64,128]{3,2,1,0:T(8,128)(2,1)} fusion(bf16[2,64,64,128]{3,2,1,0:T(8,128)(2,1)} %get-tuple-element.1773, s32[]{:T(128)} %get-tuple-element.1772, f32[]{:T(128)} %bitcast.632, f32[128]{0:T(128)S(1)} %get-tuple-element.1390, bf16[67,70,128]{2,1,0:T(8,128)(2,1)S(1)} %get-tuple-element.1421, ...), kind=kLoop, calls=%fused_computation.21.clone.1 | loop fusion | flops 88080384 | bytes 47310340 | tf_op jit(solution)/shard_map/while/body/jit(dynamic_update_index_in_dim)/dynamic_update_slice | solution.py:242
  841.7 16.7 %bitcast_dynamic-update-slice_fusion.2 = bf16[2,64,64,128]{3,2,1,0:T(8,128)(2,1)} fusion(bf16[2,64,64,128]{3,2,1,0:T(8,128)(2,1)} %get-tuple-element.1773, s32[]{:T(128)} %get-tuple-element.1772, f32[]{:T(128)} %bitcast.632, f32[128]{0:T(128)S(1)} %get-tuple-element.1390, bf16[67,70,128]{2,1,0:T(8,128)(2,1)S(1)} %get-tuple-element.1421, ...), kind=kLoop, calls=%fused_computation.21.clone.1 | loop fusion | flops 88080384 | bytes 47310340 | tf_op jit(solution)/shard_map/while/body/jit(dynamic_update_index_in_dim)/dynamic_update_slice | solution.py:242
  (526 shorter events, 196.6 us)
Async XLA Ops:
  7.2 618.5 %all-reduce.4.cloned.1.call-start = ((), (), s32[]{:S(2)}) async-start(), calls=%async_computation | async-start | bytes 1048576 | tf_op jit(solution)/shard_map/psum | solution.py:260
  9.4 20.9 %collective-permute-start = (bf16[1,2,4,3,64,128]{5,4,3,2,1,0:T(8,128)(2,1)S(1)}, bf16[1,2,4,3,64,128]{5,4,3,2,1,0:T(8,128)(2,1)S(1)}, u32[]{:S(2)}, u32[]{:S(2)}) collective-permute-start(bf16[1,2,4,3,64,128]{5,4,3,2,1,0:T(8,128)(2,1)S(1)} %maximum_bitcast_fusion.1), channel_id=1, source_target_pairs={{0,32},{4,36},{8,40},{12,44},{16,48},{20,52},{24,56},{28,60},{32,6... | collective-permute-start | bytes 1179656 | tf_op jit(solution)/shard_map/ppermute | solution.py:18
  13.4 19.5 %collective-permute-start.1 = (bf16[1,2,4,3,64,128]{5,4,3,2,1,0:T(8,128)(2,1)S(1)}, bf16[1,2,4,3,64,128]{5,4,3,2,1,0:T(8,128)(2,1)S(1)}, u32[]{:S(2)}, u32[]{:S(2)}) collective-permute-start(bf16[1,2,4,3,64,128]{5,4,3,2,1,0:T(8,128)(2,1)S(1)} %maximum_bitcast_fusion.1), channel_id=1, source_target_pairs={{0,28},{4,32},{8,36},{12,40},{16,44},{20,48},{24,52},{28,56},{32,6... | collective-permute-start | bytes 1179656 | tf_op jit(solution)/shard_map/ppermute | solution.py:18
  17.4 31.4 %collective-permute-start.2 = (bf16[1,2,4,3,64,128]{5,4,3,2,1,0:T(8,128)(2,1)S(1)}, bf16[1,2,4,3,64,128]{5,4,3,2,1,0:T(8,128)(2,1)S(1)}, u32[]{:S(2)}, u32[]{:S(2)}) collective-permute-start(bf16[1,2,4,3,64,128]{5,4,3,2,1,0:T(8,128)(2,1)S(1)} %maximum_bitcast_fusion.1), channel_id=1, source_target_pairs={{0,24},{4,28},{8,32},{12,36},{16,40},{20,44},{24,48},{28,52},{32,5... | collective-permute-start | bytes 1179656 | tf_op jit(solution)/shard_map/ppermute | solution.py:18
  23.0 30.8 %collective-permute-start.3 = (bf16[1,2,4,3,64,128]{5,4,3,2,1,0:T(8,128)(2,1)S(1)}, bf16[1,2,4,3,64,128]{5,4,3,2,1,0:T(8,128)(2,1)S(1)}, u32[]{:S(2)}, u32[]{:S(2)}) collective-permute-start(bf16[1,2,4,3,64,128]{5,4,3,2,1,0:T(8,128)(2,1)S(1)} %maximum_bitcast_fusion.1), channel_id=1, source_target_pairs={{0,20},{4,24},{8,28},{12,32},{16,36},{20,40},{24,44},{28,48},{32,5... | collective-permute-start | bytes 1179656 | tf_op jit(solution)/shard_map/ppermute | solution.py:18
  25.1 30.7 %collective-permute-start.4 = (bf16[1,2,4,3,64,128]{5,4,3,2,1,0:T(8,128)(2,1)S(1)}, bf16[1,2,4,3,64,128]{5,4,3,2,1,0:T(8,128)(2,1)S(1)}, u32[]{:S(2)}, u32[]{:S(2)}) collective-permute-start(bf16[1,2,4,3,64,128]{5,4,3,2,1,0:T(8,128)(2,1)S(1)} %maximum_bitcast_fusion.1), channel_id=1, source_target_pairs={{0,16},{4,20},{8,24},{12,28},{16,32},{20,36},{24,40},{28,44},{32,4... | collective-permute-start | bytes 1179656 | tf_op jit(solution)/shard_map/ppermute | solution.py:18
  30.3 26.8 %collective-permute-start.5 = (bf16[1,2,4,3,64,128]{5,4,3,2,1,0:T(8,128)(2,1)S(1)}, bf16[1,2,4,3,64,128]{5,4,3,2,1,0:T(8,128)(2,1)S(1)}, u32[]{:S(2)}, u32[]{:S(2)}) collective-permute-start(bf16[1,2,4,3,64,128]{5,4,3,2,1,0:T(8,128)(2,1)S(1)} %maximum_bitcast_fusion.1), channel_id=1, source_target_pairs={{0,12},{4,16},{8,20},{12,24},{16,28},{20,32},{24,36},{28,40},{32,4... | collective-permute-start | bytes 1179656 | tf_op jit(solution)/shard_map/ppermute | solution.py:18
  32.9 25.5 %collective-permute-start.6 = (bf16[1,2,4,3,64,128]{5,4,3,2,1,0:T(8,128)(2,1)S(1)}, bf16[1,2,4,3,64,128]{5,4,3,2,1,0:T(8,128)(2,1)S(1)}, u32[]{:S(2)}, u32[]{:S(2)}) collective-permute-start(bf16[1,2,4,3,64,128]{5,4,3,2,1,0:T(8,128)(2,1)S(1)} %maximum_bitcast_fusion.1), channel_id=1, source_target_pairs={{0,8},{4,12},{8,16},{12,20},{16,24},{20,28},{24,32},{28,36},{32,40... | collective-permute-start | bytes 1179656 | tf_op jit(solution)/shard_map/ppermute | solution.py:18
  53.8 11.9 %collective-permute-start.8 = (bf16[1,2,4,3,64,128]{5,4,3,2,1,0:T(8,128)(2,1)S(1)}, bf16[1,2,4,3,64,128]{5,4,3,2,1,0:T(8,128)(2,1)S(1)}, u32[]{:S(2)}, u32[]{:S(2)}) collective-permute-start(bf16[1,2,4,3,64,128]{5,4,3,2,1,0:T(8,128)(2,1)S(1)} %maximum_bitcast_fusion.1), channel_id=1, source_target_pairs={{4,0},{8,4},{12,8},{16,12},{20,16},{24,20},{28,24},{32,28},{36,32}... | collective-permute-start | bytes 1179656 | tf_op jit(solution)/shard_map/ppermute | solution.py:18
  55.8 13.0 %collective-permute-start.9 = (bf16[1,2,4,3,64,128]{5,4,3,2,1,0:T(8,128)(2,1)S(1)}, bf16[1,2,4,3,64,128]{5,4,3,2,1,0:T(8,128)(2,1)S(1)}, u32[]{:S(2)}, u32[]{:S(2)}) collective-permute-start(bf16[1,2,4,3,64,128]{5,4,3,2,1,0:T(8,128)(2,1)S(1)} %maximum_bitcast_fusion.1), channel_id=1, source_target_pairs={{8,0},{12,4},{16,8},{20,12},{24,16},{28,20},{32,24},{36,28},{40,32... | collective-permute-start | bytes 1179656 | tf_op jit(solution)/shard_map/ppermute | solution.py:18
  57.2 14.5 %collective-permute-start.10 = (bf16[1,2,4,3,64,128]{5,4,3,2,1,0:T(8,128)(2,1)S(1)}, bf16[1,2,4,3,64,128]{5,4,3,2,1,0:T(8,128)(2,1)S(1)}, u32[]{:S(2)}, u32[]{:S(2)}) collective-permute-start(bf16[1,2,4,3,64,128]{5,4,3,2,1,0:T(8,128)(2,1)S(1)} %maximum_bitcast_fusion.1), channel_id=1, source_target_pairs={{12,0},{16,4},{20,8},{24,12},{28,16},{32,20},{36,24},{40,28},{44,3... | collective-permute-start | bytes 1179656 | tf_op jit(solution)/shard_map/ppermute | solution.py:18
  58.5 19.3 %collective-permute-start.11 = (bf16[1,2,4,3,64,128]{5,4,3,2,1,0:T(8,128)(2,1)S(1)}, bf16[1,2,4,3,64,128]{5,4,3,2,1,0:T(8,128)(2,1)S(1)}, u32[]{:S(2)}, u32[]{:S(2)}) collective-permute-start(bf16[1,2,4,3,64,128]{5,4,3,2,1,0:T(8,128)(2,1)S(1)} %maximum_bitcast_fusion.1), channel_id=1, source_target_pairs={{16,0},{20,4},{24,8},{28,12},{32,16},{36,20},{40,24},{44,28},{48,3... | collective-permute-start | bytes 1179656 | tf_op jit(solution)/shard_map/ppermute | solution.py:18
  60.2 28.4 %collective-permute-start.12 = (bf16[1,2,4,3,64,128]{5,4,3,2,1,0:T(8,128)(2,1)S(1)}, bf16[1,2,4,3,64,128]{5,4,3,2,1,0:T(8,128)(2,1)S(1)}, u32[]{:S(2)}, u32[]{:S(2)}) collective-permute-start(bf16[1,2,4,3,64,128]{5,4,3,2,1,0:T(8,128)(2,1)S(1)} %maximum_bitcast_fusion.1), channel_id=1, source_target_pairs={{20,0},{24,4},{28,8},{32,12},{36,16},{40,20},{44,24},{48,28},{52,3... | collective-permute-start | bytes 1179656 | tf_op jit(solution)/shard_map/ppermute | solution.py:18
  65.7 31.3 %collective-permute-start.13 = (bf16[1,2,4,3,64,128]{5,4,3,2,1,0:T(8,128)(2,1)S(1)}, bf16[1,2,4,3,64,128]{5,4,3,2,1,0:T(8,128)(2,1)S(1)}, u32[]{:S(2)}, u32[]{:S(2)}) collective-permute-start(bf16[1,2,4,3,64,128]{5,4,3,2,1,0:T(8,128)(2,1)S(1)} %maximum_bitcast_fusion.1), channel_id=1, source_target_pairs={{24,0},{28,4},{32,8},{36,12},{40,16},{44,20},{48,24},{52,28},{56,3... | collective-permute-start | bytes 1179656 | tf_op jit(solution)/shard_map/ppermute | solution.py:18
  68.8 50.5 %collective-permute-start.14 = (bf16[1,2,4,3,64,128]{5,4,3,2,1,0:T(8,128)(2,1)S(1)}, bf16[1,2,4,3,64,128]{5,4,3,2,1,0:T(8,128)(2,1)S(1)}, u32[]{:S(2)}, u32[]{:S(2)}) collective-permute-start(bf16[1,2,4,3,64,128]{5,4,3,2,1,0:T(8,128)(2,1)S(1)} %maximum_bitcast_fusion.1), channel_id=1, source_target_pairs={{28,0},{32,4},{36,8},{40,12},{44,16},{48,20},{52,24},{56,28},{60,3... | collective-permute-start | bytes 1179656 | tf_op jit(solution)/shard_map/ppermute | solution.py:18
  71.6 49.3 %collective-permute-start.15 = (bf16[1,2,4,3,64,128]{5,4,3,2,1,0:T(8,128)(2,1)S(1)}, bf16[1,2,4,3,64,128]{5,4,3,2,1,0:T(8,128)(2,1)S(1)}, u32[]{:S(2)}, u32[]{:S(2)}) collective-permute-start(bf16[1,2,4,3,64,128]{5,4,3,2,1,0:T(8,128)(2,1)S(1)} %maximum_bitcast_fusion.1), channel_id=1, source_target_pairs={{32,0},{36,4},{40,8},{44,12},{48,16},{52,20},{56,24},{60,28},{64,3... | collective-permute-start | bytes 1179656 | tf_op jit(solution)/shard_map/ppermute | solution.py:18
  376.5 252.5 %collective-permute-start.23 = (bf16[1,2,4,3,64,128]{5,3,4,1,0,2:T(4,128)(2,1)S(1)}, bf16[1,2,4,3,64,128]{5,3,4,1,0,2:T(4,128)(2,1)S(1)}, u32[]{:S(2)}, u32[]{:S(2)}) collective-permute-start(bf16[1,2,4,3,64,128]{5,3,4,1,0,2:T(4,128)(2,1)S(1)} %maximum_bitcast_fusion), channel_id=1, source_target_pairs={{0,4},{4,8},{8,12},{12,16},{16,20},{20,24},{24,28},{28,32},{32,36}... | collective-permute-start | bytes 1179656 | tf_op jit(solution)/shard_map/ppermute | solution.py:18
  383.0 249.6 %collective-permute-start.24 = (bf16[1,2,4,3,64,128]{5,3,4,1,0,2:T(4,128)(2,1)S(1)}, bf16[1,2,4,3,64,128]{5,3,4,1,0,2:T(4,128)(2,1)S(1)}, u32[]{:S(2)}, u32[]{:S(2)}) collective-permute-start(bf16[1,2,4,3,64,128]{5,3,4,1,0,2:T(4,128)(2,1)S(1)} %maximum_bitcast_fusion), channel_id=1, source_target_pairs={{4,0},{8,4},{12,8},{16,12},{20,16},{24,20},{28,24},{32,28},{36,32}... | collective-permute-start | bytes 1179656 | tf_op jit(solution)/shard_map/ppermute | solution.py:18
  385.0 251.9 %collective-permute-start.16 = (bf16[1,2,4,3,64,128]{5,3,4,1,0,2:T(4,128)(2,1)S(1)}, bf16[1,2,4,3,64,128]{5,3,4,1,0,2:T(4,128)(2,1)}, u32[]{:S(2)}, u32[]{:S(2)}) collective-permute-start(bf16[1,2,4,3,64,128]{5,3,4,1,0,2:T(4,128)(2,1)S(1)} %maximum_bitcast_fusion), channel_id=1, source_target_pairs={{0,32},{4,36},{8,40},{12,44},{16,48},{20,52},{24,56},{28,60},{32,6... | collective-permute-start | bytes 1179656 | tf_op jit(solution)/shard_map/ppermute | solution.py:18
  389.0 254.9 %collective-permute-start.17 = (bf16[1,2,4,3,64,128]{5,3,4,1,0,2:T(4,128)(2,1)S(1)}, bf16[1,2,4,3,64,128]{5,3,4,1,0,2:T(4,128)(2,1)}, u32[]{:S(2)}, u32[]{:S(2)}) collective-permute-start(bf16[1,2,4,3,64,128]{5,3,4,1,0,2:T(4,128)(2,1)S(1)} %maximum_bitcast_fusion), channel_id=1, source_target_pairs={{0,28},{4,32},{8,36},{12,40},{16,44},{20,48},{24,52},{28,56},{32,6... | collective-permute-start | bytes 1179656 | tf_op jit(solution)/shard_map/ppermute | solution.py:18
  395.0 252.5 %collective-permute-start.18 = (bf16[1,2,4,3,64,128]{5,3,4,1,0,2:T(4,128)(2,1)S(1)}, bf16[1,2,4,3,64,128]{5,3,4,1,0,2:T(4,128)(2,1)S(1)}, u32[]{:S(2)}, u32[]{:S(2)}) collective-permute-start(bf16[1,2,4,3,64,128]{5,3,4,1,0,2:T(4,128)(2,1)S(1)} %maximum_bitcast_fusion), channel_id=1, source_target_pairs={{0,24},{4,28},{8,32},{12,36},{16,40},{20,44},{24,48},{28,52},{32,5... | collective-permute-start | bytes 1179656 | tf_op jit(solution)/shard_map/ppermute | solution.py:18
  629.0 54.6 %collective-permute-start.19 = (bf16[1,2,4,3,64,128]{5,3,4,1,0,2:T(4,128)(2,1)S(1)}, bf16[1,2,4,3,64,128]{5,3,4,1,0,2:T(4,128)(2,1)S(1)}, u32[]{:S(2)}, u32[]{:S(2)}) collective-permute-start(bf16[1,2,4,3,64,128]{5,3,4,1,0,2:T(4,128)(2,1)S(1)} %maximum_bitcast_fusion), channel_id=1, source_target_pairs={{0,20},{4,24},{8,28},{12,32},{16,36},{20,40},{24,44},{28,48},{32,5... | collective-permute-start | bytes 1179656 | tf_op jit(solution)/shard_map/ppermute | solution.py:18
  632.6 52.4 %collective-permute-start.20 = (bf16[1,2,4,3,64,128]{5,3,4,1,0,2:T(4,128)(2,1)S(1)}, bf16[1,2,4,3,64,128]{5,3,4,1,0,2:T(4,128)(2,1)S(1)}, u32[]{:S(2)}, u32[]{:S(2)}) collective-permute-start(bf16[1,2,4,3,64,128]{5,3,4,1,0,2:T(4,128)(2,1)S(1)} %maximum_bitcast_fusion), channel_id=1, source_target_pairs={{0,16},{4,20},{8,24},{12,28},{16,32},{20,36},{24,40},{28,44},{32,4... | collective-permute-start | bytes 1179656 | tf_op jit(solution)/shard_map/ppermute | solution.py:18
  636.9 49.6 %collective-permute-start.21 = (bf16[1,2,4,3,64,128]{5,3,4,1,0,2:T(4,128)(2,1)S(1)}, bf16[1,2,4,3,64,128]{5,3,4,1,0,2:T(4,128)(2,1)S(1)}, u32[]{:S(2)}, u32[]{:S(2)}) collective-permute-start(bf16[1,2,4,3,64,128]{5,3,4,1,0,2:T(4,128)(2,1)S(1)} %maximum_bitcast_fusion), channel_id=1, source_target_pairs={{0,12},{4,16},{8,20},{12,24},{16,28},{20,32},{24,36},{28,40},{32,4... | collective-permute-start | bytes 1179656 | tf_op jit(solution)/shard_map/ppermute | solution.py:18
  644.0 43.9 %collective-permute-start.22 = (bf16[1,2,4,3,64,128]{5,3,4,1,0,2:T(4,128)(2,1)S(1)}, bf16[1,2,4,3,64,128]{5,3,4,1,0,2:T(4,128)(2,1)S(1)}, u32[]{:S(2)}, u32[]{:S(2)}) collective-permute-start(bf16[1,2,4,3,64,128]{5,3,4,1,0,2:T(4,128)(2,1)S(1)} %maximum_bitcast_fusion), channel_id=1, source_target_pairs={{0,8},{4,12},{8,16},{12,20},{16,24},{20,28},{24,32},{28,36},{32,40... | collective-permute-start | bytes 1179656 | tf_op jit(solution)/shard_map/ppermute | solution.py:18
  647.5 44.0 %collective-permute-start.25 = (bf16[1,2,4,3,64,128]{5,3,4,1,0,2:T(4,128)(2,1)S(1)}, bf16[1,2,4,3,64,128]{5,3,4,1,0,2:T(4,128)(2,1)S(1)}, u32[]{:S(2)}, u32[]{:S(2)}) collective-permute-start(bf16[1,2,4,3,64,128]{5,3,4,1,0,2:T(4,128)(2,1)S(1)} %maximum_bitcast_fusion), channel_id=1, source_target_pairs={{8,0},{12,4},{16,8},{20,12},{24,16},{28,20},{32,24},{36,28},{40,32... | collective-permute-start | bytes 1179656 | tf_op jit(solution)/shard_map/ppermute | solution.py:18
  683.6 28.3 %collective-permute-start.26 = (bf16[1,2,4,3,64,128]{5,3,4,1,0,2:T(4,128)(2,1)S(1)}, bf16[1,2,4,3,64,128]{5,3,4,1,0,2:T(4,128)(2,1)S(1)}, u32[]{:S(2)}, u32[]{:S(2)}) collective-permute-start(bf16[1,2,4,3,64,128]{5,3,4,1,0,2:T(4,128)(2,1)S(1)} %maximum_bitcast_fusion), channel_id=1, source_target_pairs={{12,0},{16,4},{20,8},{24,12},{28,16},{32,20},{36,24},{40,28},{44,3... | collective-permute-start | bytes 1179656 | tf_op jit(solution)/shard_map/ppermute | solution.py:18
  685.1 30.6 %collective-permute-start.27 = (bf16[1,2,4,3,64,128]{5,3,4,1,0,2:T(4,128)(2,1)S(1)}, bf16[1,2,4,3,64,128]{5,3,4,1,0,2:T(4,128)(2,1)S(1)}, u32[]{:S(2)}, u32[]{:S(2)}) collective-permute-start(bf16[1,2,4,3,64,128]{5,3,4,1,0,2:T(4,128)(2,1)S(1)} %maximum_bitcast_fusion), channel_id=1, source_target_pairs={{16,0},{20,4},{24,8},{28,12},{32,16},{36,20},{40,24},{44,28},{48,3... | collective-permute-start | bytes 1179656 | tf_op jit(solution)/shard_map/ppermute | solution.py:18
  686.5 29.3 %collective-permute-start.28 = (bf16[1,2,4,3,64,128]{5,3,4,1,0,2:T(4,128)(2,1)S(1)}, bf16[1,2,4,3,64,128]{5,3,4,1,0,2:T(4,128)(2,1)S(1)}, u32[]{:S(2)}, u32[]{:S(2)}) collective-permute-start(bf16[1,2,4,3,64,128]{5,3,4,1,0,2:T(4,128)(2,1)S(1)} %maximum_bitcast_fusion), channel_id=1, source_target_pairs={{20,0},{24,4},{28,8},{32,12},{36,16},{40,20},{44,24},{48,28},{52,3... | collective-permute-start | bytes 1179656 | tf_op jit(solution)/shard_map/ppermute | solution.py:18
  687.9 28.0 %collective-permute-start.29 = (bf16[1,2,4,3,64,128]{5,3,4,1,0,2:T(4,128)(2,1)S(1)}, bf16[1,2,4,3,64,128]{5,3,4,1,0,2:T(4,128)(2,1)S(1)}, u32[]{:S(2)}, u32[]{:S(2)}) collective-permute-start(bf16[1,2,4,3,64,128]{5,3,4,1,0,2:T(4,128)(2,1)S(1)} %maximum_bitcast_fusion), channel_id=1, source_target_pairs={{24,0},{28,4},{32,8},{36,12},{40,16},{44,20},{48,24},{52,28},{56,3... | collective-permute-start | bytes 1179656 | tf_op jit(solution)/shard_map/ppermute | solution.py:18
  691.6 47.0 %collective-permute-start.30 = (bf16[1,2,4,3,64,128]{5,3,4,1,0,2:T(4,128)(2,1)S(1)}, bf16[1,2,4,3,64,128]{5,3,4,1,0,2:T(4,128)(2,1)S(1)}, u32[]{:S(2)}, u32[]{:S(2)}) collective-permute-start(bf16[1,2,4,3,64,128]{5,3,4,1,0,2:T(4,128)(2,1)S(1)} %maximum_bitcast_fusion), channel_id=1, source_target_pairs={{28,0},{32,4},{36,8},{40,12},{44,16},{48,20},{52,24},{56,28},{60,3... | collective-permute-start | bytes 1179656 | tf_op jit(solution)/shard_map/ppermute | solution.py:18
  711.9 41.4 %collective-permute-start.31 = (bf16[1,2,4,3,64,128]{5,3,4,1,0,2:T(4,128)(2,1)S(1)}, bf16[1,2,4,3,64,128]{5,3,4,1,0,2:T(4,128)(2,1)S(1)}, u32[]{:S(2)}, u32[]{:S(2)}) collective-permute-start(bf16[1,2,4,3,64,128]{5,3,4,1,0,2:T(4,128)(2,1)S(1)} %maximum_bitcast_fusion), channel_id=1, source_target_pairs={{32,0},{36,4},{40,8},{44,12},{48,16},{52,20},{56,24},{60,28},{64,3... | collective-permute-start | bytes 1179656 | tf_op jit(solution)/shard_map/ppermute | solution.py:18
  (131 other events, 845.1 us)
Sparse Core Ops, SparseCore 0:
  481.8 143.7 all-reduce.3
where the time goes:
time: 875 us; the launch traced here: 866 us
  waiting for transfers between devices  310 us (35%)
  other arithmetic  160 us (18%)
  loops' own time  110 us (13%)
  starting transfers between devices  82.6 us (9%)
  blocking collectives  82.6 us (9%)
  local copies, waits for them, and re-layouts  56.4 us (6%)
  matrix products  48.5 us (6%)
  between operations  15.3 us (2%)
    ppermute x32, waiting for transfers between devices, passed_along(): return lax.ppermute(value, axis, pairs)  167 us
    psum x1, waiting for transfers between devices, local(): lax.psum((grad_sums[0], grad_sums[1], grad_sums[2], grad_sums[3], grad_su...  143 us
    psum x1, blocking collectives, local(): lax.psum((grad_sums[0], grad_sums[1], grad_sums[2], grad_sums[3], grad_su...  82.6 us
    ppermute x32, starting transfers between devices, passed_along(): return lax.ppermute(value, axis, pairs)  82.5 us
    another operation x1, loops' own time, local(): lax.scan(first_step, grad_sums, jnp.arange(slot_count))  63 us
    another operation x1, loops' own time, local(): outputs = [lax.map(second_step, jnp.arange(slot_count))]  47.2 us
    reduce_sum x6, other arithmetic, kernel_terms(): line_terms.append(jnp.sum(grad_values * window, axis=(0, 1)))  47.1 us
    dynamic_update_slice x2, other arithmetic, local(): lax.scan(first_step, grad_sums, jnp.arange(slot_count))  33.4 us
  transfers between devices with their start and end apart: 33, of which 18 were waited for; matrix products, arithmetic and copies ran while one was open for 1% of the time, Pallas kernels for 0%

commit v1 on v0

v1 whole, which is shorter than its diff:
```python
from functools import partial
import math

import jax
import jax.numpy as jnp
from jax import lax
from jax.experimental import pallas as pl
from jax.experimental.pallas import tpu as pltpu
from jax.sharding import PartitionSpec as P


EPSILON = 1e-06
BF = jnp.bfloat16
F32 = jnp.float32
PITCH = 80
LEFT = 5
C0 = math.sqrt(2.0 / math.pi)
C1 = 0.044715
VMEM = pltpu.VMEM
LIMIT = 60 * 1024 * 1024


RB = 8
UN = 2


def gelu_pair(h, ga):
    sq = h * h
    t = jnp.tanh(h * (C0 + (C0 * C1) * sq))
    s = 0.5 + 0.5 * t
    act = h * s
    slope = s + (act - act * s) * (2 * C0 + (6 * C0 * C1) * sq)
    return act.astype(BF), (ga * slope).astype(BF)


def vspec():
    return pl.BlockSpec(memory_space=pltpu.VMEM)


def sspec():
    return pl.BlockSpec(memory_space=pltpu.SMEM)


def call(kernel, outs, scratch, args, smem, flops=0, bytes_accessed=0, blocks=None, alias=None):
    blocks = blocks or {}
    specs = [
        sspec() if i < smem else blocks.get(i, vspec()) for i in range(len(args))
    ]
    return pl.pallas_call(
        kernel,
        out_shape=outs,
        grid=(1,) if blocks else (),
        in_specs=specs,
        out_specs=jax.tree.map(lambda _: vspec(), outs),
        scratch_shapes=scratch,
        input_output_aliases=alias or {},
        compiler_params=pltpu.CompilerParams(vmem_limit_bytes=LIMIT),
        cost_estimate=pl.CostEstimate(
            flops=flops, bytes_accessed=bytes_accessed, transcendentals=0
        ),
    )(*args)


def pack_sides(nb, west_of, east_of, to_prev, to_next, wide):
    position = lax.axis_index("tile")
    for slot in range(2):
        s = 2 * position + slot
        east_prev = jnp.bool_(False)
        east_next = jnp.bool_(False)
        for d in (3, 5, 7):
            e = nb[slot, d]
            east_prev = east_prev | ((e >= 0) & (e < s))
            east_next = east_next | (e > s)
        wide[0] = west_of(slot).astype(F32).reshape(512, 128)
        wide[1] = east_of(slot).astype(F32).reshape(512, 128)
        for j in range(3):
            west = wide[0, pl.ds(j, 64, stride=8), :]
            east = wide[1, pl.ds(5 + j, 64, stride=8), :]
            to_prev[slot, j] = jnp.where(east_prev, east, west).astype(BF)
            to_next[slot, j] = jnp.where(east_next, east, west).astype(BF)


def sides_kernel(nb, west, east, to_prev, to_next, wide):
    pack_sides(nb, lambda s: west[s], lambda s: east[s], to_prev, to_next, wide)


def pack_ends(nb, above, below, from_prev, from_next, to_prev, to_next):
    position = lax.axis_index("tile")
    for slot, out, entry in ((0, to_prev, -1), (1, to_next, 1)):
        s = 2 * position + slot
        north = nb[slot, 0] == s + entry
        for i in range(3):
            top = above[slot, i].astype(F32)
            low = below[slot, 1 + i].astype(F32)
            out[64 * i : 64 * i + 64, :] = jnp.where(north, top, low).astype(BF)
        for side, strip in ((0, from_prev), (1, from_next)):
            for j in range(3):
                for edge in range(2):
                    at = 192 + 8 * (edge + 2 * (j + 3 * side))
                    out[at : at + 8, :] = strip[1 - slot, j, 56 * edge : 56 * edge + 8, :]


def window(shape, *index):
    return pl.BlockSpec(shape, lambda i: index)


SIDES = jax.ShapeDtypeStruct((2, 3, 64, 128), BF)
ENDS = jax.ShapeDtypeStruct((288, 128), BF)


def sides_of(nb, x):
    block = (2, 64, 8, 128)
    return call(
        sides_kernel,
        (SIDES, SIDES),
        [VMEM((2, 512, 128), F32)],
        (nb, x, x),
        1,
        blocks={1: window(block, 0, 0, 0, 0), 2: window(block, 0, 0, 7, 0)},
    )


def across(to_prev, to_next):
    columns = lax.axis_size("tile") // 4
    onward = [(4 * c + p, 4 * c + 7 - p) for c in range(columns - 1) for p in range(4)]
    back = [(b, a) for a, b in onward]
    onto = lax.ppermute(to_next, "tile", onward)
    return onto, lax.ppermute(to_prev, "tile", back)


def along(nb, x, from_prev, from_next):
    block = (2, 4, 64, 128)
    end_prev, end_next = call(
        pack_ends,
        (ENDS, ENDS),
        [],
        (nb, x, x, from_prev, from_next),
        1,
        blocks={1: window(block, 0, 0, 0, 0), 2: window(block, 0, 15, 0, 0)},
    )
    columns = lax.axis_size("tile") // 4
    down = [(4 * c + p, 4 * c + p + 1) for c in range(columns) for p in range(3)]
    up = [(b, a) for a, b in down]
    onto = lax.ppermute(end_next, "tile", down)
    return onto, lax.ppermute(end_prev, "tile", up)


def fill(nb, x, from_prev, from_next, chain_prev, chain_next, padded):
    position = lax.axis_index("tile")
    column = position // 4
    place = position % 4
    for slot in range(2):
        s = 2 * position + slot
        flat = padded.at[slot].reshape(70 * PITCH, 128)
        chain = chain_next if slot else chain_prev

        def body(i, carry):
            padded[slot, 3 + i, 8:72, :] = x[slot, i].astype(F32)
            return carry

        lax.fori_loop(0, 64, body, 0)
        for d, row, source in ((0, 0, 61), (1, 67, 0)):
            e = nb[slot, d]
            own = e == 2 * position + 1 - slot
            for i in range(3):
                mine = x[1 - slot, source + i].astype(F32)
                other = chain[64 * i : 64 * i + 64, :].astype(F32)
                value = jnp.where(own, mine, other)
                padded[slot, row + i, 8:72, :] = jnp.where(e >= 0, value, 0.0)
        for d, col in ((2, LEFT), (3, 72)):
            e = nb[slot, d]
            for j in range(3):
                value = jnp.where(
                    e < s,
                    from_prev[1 - slot, j].astype(F32),
                    from_next[1 - slot, j].astype(F32),
                )
                flat[pl.ds(3 * PITCH + col + j, 64, stride=PITCH), :] = jnp.where(
                    e >= 0, value, 0.0
                )
        for d, row, col, edge in (
            (4, 0, LEFT, 1),
            (5, 0, 72, 1),
            (6, 67, LEFT, 0),
            (7, 67, 72, 0),
        ):
            e = nb[slot, d]
            prev = e < s
            facing = jnp.where(prev, 8 * column - 2 - 2 * place, 8 * column + 14 - 2 * place)
            near = e == facing + slot
            for j in range(3):
                direct = jnp.where(
                    prev,
                    from_prev[slot, j, 56 * edge : 56 * edge + 8].astype(F32),
                    from_next[slot, j, 56 * edge : 56 * edge + 8].astype(F32),
                )
                at_prev = 192 + 8 * (edge + 2 * j)
                at_next = at_prev + 48
                relayed = jnp.where(
                    prev,
                    chain[at_prev : at_prev + 8].astype(F32),
                    chain[at_next : at_next + 8].astype(F32),
                )
                value = jnp.where(e >= 0, jnp.where(near, direct, relayed), 0.0)
                first = 5 if edge else 0
                for i in range(3):
                    at = (row + i) * PITCH + col + j
                    flat[at : at + 1, :] = value[first + i : first + i + 1]


def taps(padded, slot, kb, start, emit, flipped):
    def group(n, carry):
        row0 = 8 * (n // 4)
        col0 = pl.multiple_of(16 * (n % 4), 16)
        acc = [start(row0 + r, col0) for r in range(8)]
        for b in range(7):
            kk = [
                kb[(6 - a) * 7 + 6 - b] if flipped else kb[a * 7 + b] for a in range(7)
            ]
            for r in range(14):
                halves = [
                    padded[slot, row0 + r, pl.ds(col0 + (LEFT + b + 8 * h), 8), :]
                    for h in range(2)
                ]
                for a in range(7):
                    if 0 <= r - a < 8:
                        acc[r - a] = [acc[r - a][h] + halves[h] * kk[a] for h in range(2)]
        for r in range(8):
            emit(row0 + r, col0, acc[r])
        return carry

    lax.fori_loop(0, 32, group, 0)


def first_kernel(
    nb, ocean, x, from_prev, from_next, chain_prev, chain_next, cot, kb, cbias, wu, wd, wut, hbias,
    grad, to_prev, to_next, flat,
    padded, conv, nterm, aterm, sums, wide,
):
    fill(nb, x, from_prev, from_next, chain_prev, chain_next, padded)
    nterm[...] = jnp.zeros_like(nterm)
    aterm[...] = jnp.zeros_like(aterm)
    sums[...] = jnp.zeros_like(sums)
    ones = jnp.ones((16, 64 * RB), BF)

    def tile(slot):
        cb = jnp.broadcast_to(cbias[...], (8, 128))

        def keep(row, col0, value):
            for h in range(2):
                conv[row, pl.ds(col0 + 8 * h, 8), :] = value[h]

        taps(padded, slot, kb, lambda r, c: [cb, cb], keep, False)

        def block(at):
            value = conv[pl.ds(at, RB)].reshape(64 * RB, 128)
            ct = cot[slot, pl.ds(at, RB)].reshape(64 * RB, 128)
            mean = jnp.mean(value, -1, keepdims=True)
            centred = value - mean
            variance = jnp.mean(centred * centred, -1, keepdims=True)
            inverse = lax.rsqrt(variance + EPSILON)
            normed = centred * inverse
            nb16 = normed.astype(BF)
            left = jnp.concatenate([nb16.T, ones], 0)
            ctt = ct.T
            q = 0.0
            for part in range(2):
                cols = slice(256 * part, 256 * part + 256)
                h = jnp.dot(nb16, wu[:, cols], preferred_element_type=F32) + hbias[:, cols]
                ga = jnp.dot(ct, wd[:, cols], preferred_element_type=F32)
                act, gp = gelu_pair(h, ga)
                nterm[:, cols] += jnp.dot(left, gp, preferred_element_type=F32)
                aterm[:, cols] += jnp.dot(ctt, act, preferred_element_type=F32)
                q = q + jnp.dot(gp, wut[cols, :], preferred_element_type=F32)
            qm = q[:, 128:]
            q = q[:, :128]
            cross = jnp.mean(q * normed, -1, keepdims=True)
            gc = (inverse * (q - qm - normed * cross)).astype(BF)
            grad[slot, pl.ds(at, RB)] = gc.reshape(RB, 64, 128)
            sums[0:8] += jnp.sum(ct.astype(F32).reshape(8 * RB, 8, 128), 0)
            sums[8:16] += jnp.sum(gc.astype(F32).reshape(8 * RB, 8, 128), 0)

        def rows(i, carry):
            for u in range(UN):
                block(pl.multiple_of(RB * (UN * i + u), RB))
            return carry

        lax.fori_loop(0, 64 // (RB * UN), rows, 0)

    def step(slot, carry):
        pl.when(ocean[slot] > 0)(lambda: tile(slot))
        return carry

    lax.fori_loop(0, 2, step, 0)
    pack_sides(
        nb, lambda s: grad[s, :, 0:8, :], lambda s: grad[s, :, 56:64, :], to_prev, to_next, wide
    )
    for k in range(4):
        cols = slice(128 * k, 128 * k + 128)
        flat[cols] = nterm[0:128, cols]
        flat[512 + 128 * k : 640 + 128 * k] = aterm[:, cols]
        flat[1024 + k : 1025 + k] = nterm[128:129, cols]
    flat[1028:1029] = jnp.sum(sums[0:8], 0, keepdims=True)
    flat[1029:1030] = jnp.sum(sums[8:16], 0, keepdims=True)
    flat[1030:1152] = jnp.zeros((122, 128), F32)


def third_kernel(
    nb, ocean, flat_in, x, from_prev, from_next, chain_prev, chain_next, grad, flat,
    padded, gsc, kacc,
):
    fill(nb, x, from_prev, from_next, chain_prev, chain_next, padded)
    kacc[...] = jnp.zeros_like(kacc)

    def tile(slot):
        def widen(i, carry):
            gsc[i] = grad[slot, i].astype(F32)
            return carry

        lax.fori_loop(0, 64, widen, 0)

        def kgroup(n, carry):
            row0 = 8 * (n // 4)
            col0 = pl.multiple_of(16 * (n % 4), 16)
            g = [
                [gsc[row0 + r, pl.ds(col0 + 8 * h, 8), :] for h in range(2)] for r in range(8)
            ]
            for b in range(7):
                acc = [kacc[a * 7 + b] for a in range(7)]
                for r in range(14):
                    for h in range(2):
                        v = padded[slot, row0 + r, pl.ds(col0 + (LEFT + b + 8 * h), 8), :]
                        for a in range(7):
                            if 0 <= r - a < 8:
                                acc[a] = acc[a] + v * g[r - a][h]
                for a in range(7):
                    kacc[a * 7 + b] = acc[a]
            return carry

        lax.fori_loop(0, 32, kgroup, 0)

    def step(slot, carry):
        pl.when(ocean[slot] > 0)(lambda: tile(slot))
        return carry

    lax.fori_loop(0, 2, step, 0)
    flat[...] = flat_in[...]
    flat[1032:1081] = jnp.sum(kacc[...], 1)


def second_kernel(
    nb, ocean, g, from_prev, from_next, chain_prev, chain_next, cot, kb, out, padded
):
    fill(nb, g, from_prev, from_next, chain_prev, chain_next, padded)

    def step(slot, carry):
        def start(row, col0):
            both = cot[slot, row, pl.ds(col0, 16), :].astype(F32)
            return [both[:8], both[8:]]

        def emit(row, col0, value):
            both = jnp.concatenate(value, 0).astype(BF)
            out[slot, row, pl.ds(col0, 16), :] = both

        @pl.when(ocean[slot] > 0)
        def _():
            taps(padded, slot, kb, start, emit, True)

        @pl.when(ocean[slot] <= 0)
        def _():
            out[slot] = jnp.zeros((64, 64, 128), BF)

        return carry

    lax.fori_loop(0, 2, step, 0)


def whole(
    fields, cotangent, is_ocean, neighbours, kernel, conv_bias, ln_gain, ln_bias,
    w_up, up_bias, w_down, down_bias, layer_scale,
):
    x = fields[0]
    cot = cotangent[0]
    kb = jnp.broadcast_to(kernel.reshape(49, 1, 128), (49, 8, 128))
    upf = w_up.astype(F32)
    downf = w_down.astype(F32)
    gained = upf * ln_gain[:, None]
    wu = gained.astype(BF)
    wd = (downf * layer_scale[None, :]).T.astype(BF)
    mean_row = jnp.mean(gained, 0)
    wut = jnp.concatenate(
        [gained.T, jnp.broadcast_to(mean_row[:, None], (512, 128))], 1
    ).astype(BF)
    hbias = (up_bias + jnp.dot(ln_bias, upf, precision="highest"))[None]
    sides = across(*sides_of(neighbours, x))
    halos = (*sides, *along(neighbours, x, *sides))
    sd = jax.ShapeDtypeStruct
    pad = VMEM((2, 70, PITCH, 128), F32)
    grad, to_prev, to_next, flat = call(
        first_kernel,
        (sd((2, 64, 64, 128), BF), SIDES, SIDES, sd((1152, 128), F32)),
        [
            pad,
            VMEM((64, 64, 128), F32),
            VMEM((144, 512), F32),
            VMEM((128, 512), F32),
            VMEM((16, 128), F32),
            VMEM((2, 512, 128), F32),
        ],
        (neighbours, is_ocean, x, *halos, cot, kb, conv_bias[None], wu, wd, wut, hbias),
        2,
        flops=2 * 10**10,
        bytes_accessed=10**7,
    )
    sides = across(to_prev, to_next)
    flat = call(
        third_kernel,
        sd((1152, 128), F32),
        [pad, VMEM((64, 64, 128), F32), VMEM((49, 8, 128), F32)],
        (neighbours, is_ocean, flat, x, *halos, grad),
        2,
        flops=10**10,
        bytes_accessed=10**7,
        alias={2: 0},
    )
    halos_g = (*sides, *along(neighbours, grad, *sides))
    out = call(
        second_kernel,
        sd((2, 64, 64, 128), BF),
        [pad],
        (neighbours, is_ocean, grad, *halos_g, cot, kb),
        2,
        flops=10**10,
        bytes_accessed=10**7,
    )
    n = lax.axis_size("tile") * lax.axis_size("dp")
    axes = ("tile", "dp")
    got = lax.all_to_all(flat.reshape(n, 1, 1152 * 128 // n), axes, 0, 0, tiled=True)
    mine = jnp.sum(got, 0)
    spread = jnp.broadcast_to(mine[None], (n, *mine.shape))
    flat = lax.all_to_all(spread, axes, 0, 0, tiled=True).reshape(1152, 128)
    scale = 1.0 / math.sqrt(
        fields.shape[0]
        * lax.axis_size("dp")
        * fields.shape[1]
        * lax.axis_size("tile")
        * fields.shape[2] ** 2
    )
    row = sd((1, 128), F32)
    rows = jnp.stack([ln_gain, ln_bias, layer_scale, down_bias])
    done = call(
        partial(finish_kernel, scale),
        (
            sd((7, 7, 128), F32),
            row,
            row,
            row,
            sd((128, 512), F32),
            sd((1, 512), F32),
            sd((512, 128), F32),
            row,
            row,
        ),
        [],
        (flat, rows, w_up, w_down),
        0,
    )
    done = [d[0] if d.shape[0] == 1 else d for d in done]
    return (out[None], *done)


def finish_kernel(
    scale, flat, rows, w_up, w_down,
    g_kernel, g_conv_bias, g_ln_gain, g_ln_bias, g_w_up, g_up_bias, g_w_down, g_down_bias,
    g_layer_scale,
):
    square = (128, 128)
    gain = jnp.broadcast_to(rows[0:1], square).T
    bias = jnp.broadcast_to(rows[1:2], square).T
    layer = rows[2:3]
    cot_sum = flat[1028:1029] * scale
    gains = jnp.zeros(square, F32)
    biases = jnp.zeros(square, F32)
    layers = jnp.zeros(square, F32)
    for k in range(4):
        cols = slice(128 * k, 128 * k + 128)
        upper = w_up[:, cols].astype(F32)
        n = flat[cols] * scale
        a = flat[512 + 128 * k : 640 + 128 * k].T * scale
        up = flat[1024 + k : 1025 + k] * scale
        g_w_up[:, cols] = n * gain + bias * up
        g_up_bias[:, cols] = up
        g_w_down[cols, :] = a * layer
        gains = gains + n * upper
        biases = biases + upper * up
        layers = layers + a * w_down[cols, :].astype(F32)
    g_ln_gain[...] = jnp.sum(gains.T, 0, keepdims=True)
    g_ln_bias[...] = jnp.sum(biases.T, 0, keepdims=True)
    g_layer_scale[...] = jnp.sum(layers, 0, keepdims=True) + rows[3:4] * cot_sum
    g_down_bias[...] = layer * cot_sum
    g_conv_bias[...] = flat[1029:1030] * scale
    for i in range(7):
        g_kernel[i] = flat[1032 + 7 * i : 1039 + 7 * i] * scale


def solution(mesh):
    placed = (
        P("dp", "tile", None, None, None),
        P("dp", "tile", None, None, None),
        P("tile"),
        P("tile", None),
    ) + (P(),) * 9
    return jax.shard_map(
        whole,
        mesh=mesh,
        in_specs=placed,
        out_specs=(P("dp", "tile", None, None, None),) + (P(),) * 9,
        check_vma=False,
    )
```

time: 875 us -> 159 us (0.18); the launches traced: 866 us -> 159 us
  waiting for transfers between devices: 310 us -> 14.4 us
  other arithmetic: 160 us -> 3.19 us
  loops' own time: 110 us -> 0 us
  Pallas kernels: 0 us -> 94.1 us
  blocking collectives: 82.6 us -> 0 us
  local copies, waits for them, and re-layouts: 56.4 us -> 6.33 us
  matrix products: 48.5 us -> 0.15 us
  starting transfers between devices: 82.6 us -> 39.5 us
  between operations: 15.3 us -> 0.93 us
    ppermute x32 -> x8, waiting for transfers between devices: 167 us -> 14.4 us  [the longest x2 6.39 us: across(): onto = lax.ppermute(to_next, 'tile', onward)]
    psum x1 -> x0, waiting for transfers between devices: 143 us -> none  [local(): lax.psum((grad_sums[0], grad_sums[1], grad_sums[2], grad_sums[3], grad_su...]
    another operation x2 -> x0, loops' own time: 110 us -> none  [the longest x1 63 us: local(): lax.scan(first_step, grad_sums, jnp.arange(slot_count))]
    pallas_call x0 -> x7, Pallas kernels: none -> 94.1 us  [call(): pl.pallas_call(kernel, out_shape=outs, grid=(1,) if blocks else (), in_sp...]
    reduce_sum x14 -> x2, other arithmetic: 88.3 us -> 0.53 us  [the longest x1 0.38 us: whole(): mine = jnp.sum(got, 0)]
    psum x1 -> x0, blocking collectives: 82.6 us -> none  [local(): lax.psum((grad_sums[0], grad_sums[1], grad_sums[2], grad_sums[3], grad_su...]
    ppermute x32 -> x8, starting transfers between devices: 82.5 us -> 23.7 us  [the longest x2 12.4 us: across(): onto = lax.ppermute(to_next, 'tile', onward)]
    dot_general x12 -> x1, matrix products: 48.5 us -> 0.15 us  [whole(): hbias = (up_bias + jnp.dot(ln_bias, upf, precision='highest'))[None]]
  transfers between devices with their start and end apart: 33 -> 10, of which waited for: 18 -> 4; matrix products, arithmetic and copies ran while one was open for 1% -> 4% of each run, Pallas kernels for 0% -> 14%
where the time goes in v1:
time: 159 us
  Pallas kernels  94.1 us (59%)
  starting transfers between devices  39.5 us (25%)
  waiting for transfers between devices  14.4 us (9%)
  local copies, waits for them, and re-layouts  6.33 us (4%)
  other arithmetic  3.19 us (2%)
    pallas_call x7, Pallas kernels, call(): pl.pallas_call(kernel, out_shape=outs, grid=(1,) if blocks else (), in_sp...  94.1 us
    ppermute x2, starting transfers between devices, across(): onto = lax.ppermute(to_next, 'tile', onward)  12.4 us
    all_to_all x1, starting transfers between devices, whole(): lax.all_to_all(flat.reshape(n, 1, 1152 * 128 // n), axes, 0, 0, tiled=True)  7.91 us
    all_to_all x1, starting transfers between devices, whole(): flat = lax.all_to_all(spread, axes, 0, 0, tiled=True).reshape(1152, 128)  7.9 us
    ppermute x2, waiting for transfers between devices, across(): onto = lax.ppermute(to_next, 'tile', onward)  6.39 us
    ppermute x2, waiting for transfers between devices, across(): return (onto, lax.ppermute(to_prev, 'tile', back))  5.38 us
    ppermute x2, starting transfers between devices, along(): return (onto, lax.ppermute(end_prev, 'tile', up))  4.81 us
    ppermute x2, starting transfers between devices, along(): onto = lax.ppermute(end_next, 'tile', down)  3.82 us
  transfers between devices with their start and end apart: 10, of which 4 were waited for; matrix products, arithmetic and copies ran while one was open for 4% of the time, Pallas kernels for 14%

profile of v1, /device:TPU:1, one launch (start us, length us, event | category | flops | bytes accessed | tf_op | source)
XLA Modules:
  0.0 158.5 jit_solution(5364916168962162579)
XLA Ops:
  0.7 2.0 %shard_map.204 = (bf16[2,3,64,128]{3,2,1,0:T(8,128)(2,1)}, bf16[2,3,64,128]{3,2,1,0:T(8,128)(2,1)}) custom-call(s32[2,8]{1,0:T(2,128)} %nb.11, bf16[2,64,64,128]{3,2,1,0:T(8,128)(2,1)} %bitcast.25, bf16[2,64,64,128]{3,2,1,0:T(8,128)(2,1)} %bitcast.26), custom_call_target="tpu_custom_call" | custom-call | tf_op jit(solution)/shard_map/pallas_call | solution.py:49
  2.7 7.0 %collective-permute-start = (bf16[2,3,64,128]{3,2,1,0:T(8,128)(2,1)}, bf16[2,3,64,128]{3,2,1,0:T(8,128)(2,1)S(1)}, u32[]{:S(2)}, u32[]{:S(2)}) collective-permute-start(bf16[2,3,64,128]{3,2,1,0:T(8,128)(2,1)} %get-tuple-element.29), channel_id=1, source_target_pairs={{0,28},{4,24},{8,20},{12,16},{16,44},{20,40},{24,36},{28,32},{32,6... | collective-permute-start | bytes 294920 | tf_op jit(solution)/shard_map/ppermute | solution.py:127
  9.7 1.3 collective-permute-start.1
  11.5 0.7 fusion.2.wd
  12.4 0.8 copy.29.wu
  13.8 3.5 %collective-permute-done.1.from_next = bf16[2,3,64,128]{3,2,1,0:T(8,128)(2,1)S(1)} collective-permute-done((bf16[2,3,64,128]{3,2,1,0:T(8,128)(2,1)}, bf16[2,3,64,128]{3,2,1,0:T(8,128)(2,1)S(1)}, u32[]{:S(2)}, u32[]{:S(2)}) %collective-permute-start.1) | collective-permute-done | bytes 98336 | tf_op jit(solution)/shard_map/ppermute | solution.py:128
  17.3 0.6 copy-done.4
  17.9 1.8 %shard_map.205 = (bf16[288,128]{1,0:T(8,128)(2,1)}, bf16[288,128]{1,0:T(8,128)(2,1)}) custom-call(s32[2,8]{1,0:T(2,128)} %nb.11, bf16[2,64,64,128]{3,2,1,0:T(8,128)(2,1)} %bitcast.27, bf16[2,64,64,128]{3,2,1,0:T(8,128)(2,1)} %bitcast.28, bf16[2,3,64,128]{3,2,1,0:T(8,128)(2,1)} %copy-done.3, bf16[2,3,64,128]{3,2,1,0:T(8,128)(2,1)} %copy-done.4), custom_call_target="tpu_custom_call" | custom-call | tf_op jit(solution)/shard_map/pallas_call | solution.py:49
  19.7 1.9 %collective-permute-start.2 = (bf16[288,128]{1,0:T(8,128)(2,1)}, bf16[288,128]{1,0:T(8,128)(2,1)S(1)}, u32[]{:S(2)}, u32[]{:S(2)}) collective-permute-start(bf16[288,128]{1,0:T(8,128)(2,1)} %get-tuple-element.31), channel_id=1, source_target_pairs={{0,4},{4,8},{8,12},{16,20},{20,24},{24,28},{32,36},{36,40},{40,44}... | collective-permute-start | bytes 221192 | tf_op jit(solution)/shard_map/ppermute | solution.py:144
  21.6 2.4 %collective-permute-start.3 = (bf16[288,128]{1,0:T(8,128)(2,1)}, bf16[288,128]{1,0:T(8,128)(2,1)S(1)}, u32[]{:S(2)}, u32[]{:S(2)}) collective-permute-start(bf16[288,128]{1,0:T(8,128)(2,1)} %get-tuple-element.32), channel_id=1, source_target_pairs={{4,0},{8,4},{12,8},{20,16},{24,20},{28,24},{36,32},{40,36},{44,40}... | collective-permute-start | bytes 221192 | tf_op jit(solution)/shard_map/ppermute | solution.py:145
  24.2 0.7 pad_maximum_fusion.wut
  24.9 2.6 %collective-permute-done.3.chain_next = bf16[288,128]{1,0:T(8,128)(2,1)S(1)} collective-permute-done((bf16[288,128]{1,0:T(8,128)(2,1)}, bf16[288,128]{1,0:T(8,128)(2,1)S(1)}, u32[]{:S(2)}, u32[]{:S(2)}) %collective-permute-start.3) | collective-permute-done | bytes 73760 | tf_op jit(solution)/shard_map/ppermute | solution.py:145
  27.5 0.7 broadcast_in_dim.33.kb
  28.2 46.0 %shard_map.206 = (bf16[2,64,64,128]{3,2,1,0:T(8,128)(2,1)}, bf16[2,3,64,128]{3,2,1,0:T(8,128)(2,1)}, bf16[2,3,64,128]{3,2,1,0:T(8,128)(2,1)}, f32[1152,128]{1,0:T(8,128)}) custom-call(s32[2,8]{1,0:T(2,128)} %nb.11, s32[2]{0:T(128)} %ocean.5, bf16[2,64,64,128]{3,2,1,0:T(8,128)(2,1)} %bitcast.29, bf16[2,3,64,128]{3,2,1,0:T(8,128)(2,1)} %copy-done.3, ...), custom_call_target="tpu_custom_call" | custom-call | flops 20000000000 | bytes 10000000 | tf_op jit(solution)/shard_map/pallas_call | solution.py:49
  74.2 19.7 %shard_map.209 = f32[1152,128]{1,0:T(8,128)} custom-call(s32[2,8]{1,0:T(2,128)} %nb.11, s32[2]{0:T(128)} %ocean.5, f32[1152,128]{1,0:T(8,128)} %get-tuple-element.38.flat_in, bf16[2,64,64,128]{3,2,1,0:T(8,128)(2,1)} %bitcast.30, bf16[2,3,64,128]{3,2,1,0:T(8,128)(2,1)} %copy-done.3, ...), custom_call_target="tpu_custom_call", output_to_operand_aliasing={{}: (2, {})} | custom-call | flops 10000000000 | bytes 10000000 | tf_op jit(solution)/shard_map/pallas_call | solution.py:49
  93.9 7.9 %all-to-all-start = ((f32[128,1,1152]{2,1,0:T(1,128)}), f32[128,1,1152]{2,1,0:T(1,128)S(1)}, u32[]{:S(2)}, u32[]{:S(2)}) async-start(f32[128,1,1152]{2,1,0:T(1,128)} %bitcast.33), calls=%async_computation | async-start | bytes 1179648 | tf_op jit(solution)/shard_map/all_to_all | solution.py:438
  101.9 5.4 %collective-permute-start.4 = (bf16[2,3,64,128]{3,2,1,0:T(8,128)(2,1)S(1)}, bf16[2,3,64,128]{3,2,1,0:T(8,128)(2,1)S(1)}, u32[]{:S(2)}, u32[]{:S(2)}) collective-permute-start(bf16[2,3,64,128]{3,2,1,0:T(8,128)(2,1)S(1)} %copy-done.14), channel_id=1, source_target_pairs={{0,28},{4,24},{8,20},{12,16},{16,44},{20,40},{24,36},{28,32},{32,6... | collective-permute-start | bytes 294920 | tf_op jit(solution)/shard_map/ppermute | solution.py:127
  107.3 1.3 collective-permute-start.5
  108.6 6.4 %collective-permute-done.4.from_prev = bf16[2,3,64,128]{3,2,1,0:T(8,128)(2,1)S(1)} collective-permute-done((bf16[2,3,64,128]{3,2,1,0:T(8,128)(2,1)S(1)}, bf16[2,3,64,128]{3,2,1,0:T(8,128)(2,1)S(1)}, u32[]{:S(2)}, u32[]{:S(2)}) %collective-permute-start.4) | collective-permute-done | bytes 98336 | tf_op jit(solution)/shard_map/ppermute | solution.py:127
  115.0 1.8 %collective-permute-done.5.from_next = bf16[2,3,64,128]{3,2,1,0:T(8,128)(2,1)S(1)} collective-permute-done((bf16[2,3,64,128]{3,2,1,0:T(8,128)(2,1)S(1)}, bf16[2,3,64,128]{3,2,1,0:T(8,128)(2,1)S(1)}, u32[]{:S(2)}, u32[]{:S(2)}) %collective-permute-start.5) | collective-permute-done | bytes 98336 | tf_op jit(solution)/shard_map/ppermute | solution.py:128
  116.8 0.6 copy-done.6
  117.5 1.8 %shard_map.207 = (bf16[288,128]{1,0:T(8,128)(2,1)}, bf16[288,128]{1,0:T(8,128)(2,1)}) custom-call(s32[2,8]{1,0:T(2,128)} %nb.11, bf16[2,64,64,128]{3,2,1,0:T(8,128)(2,1)} %get-tuple-element.33.above.below.g.grad, bf16[2,64,64,128]{3,2,1,0:T(8,128)(2,1)} %get-tuple-element.33.above.below.g.grad, bf16[2,3,64,128]{3,2,1,0:T(8,128)(2,1)} %copy-done.5, ...), custom_call_target="tpu_custom_call" | custom-call | tf_op jit(solution)/shard_map/pallas_call | solution.py:49
  119.2 1.9 %collective-permute-start.6 = (bf16[288,128]{1,0:T(8,128)(2,1)}, bf16[288,128]{1,0:T(8,128)(2,1)S(1)}, u32[]{:S(2)}, u32[]{:S(2)}) collective-permute-start(bf16[288,128]{1,0:T(8,128)(2,1)} %get-tuple-element.36), channel_id=1, source_target_pairs={{0,4},{4,8},{8,12},{16,20},{20,24},{24,28},{32,36},{36,40},{40,44}... | collective-permute-start | bytes 221192 | tf_op jit(solution)/shard_map/ppermute | solution.py:144
  121.2 2.4 %collective-permute-start.7 = (bf16[288,128]{1,0:T(8,128)(2,1)}, bf16[288,128]{1,0:T(8,128)(2,1)S(1)}, u32[]{:S(2)}, u32[]{:S(2)}) collective-permute-start(bf16[288,128]{1,0:T(8,128)(2,1)} %get-tuple-element.37), channel_id=1, source_target_pairs={{4,0},{8,4},{12,8},{20,16},{24,20},{28,24},{36,32},{40,36},{44,40}... | collective-permute-start | bytes 221192 | tf_op jit(solution)/shard_map/ppermute | solution.py:145
  123.6 0.6 pad_maximum_fusion.1.rows
  124.6 1.1 broadcast_in_dim.38
  125.7 7.9 %all-to-all-start.1 = ((f32[128,1,1152]{2,1,0:T(1,128)}), f32[128,1,1152]{2,1,0:T(1,128)S(1)}, u32[]{:S(2)}, u32[]{:S(2)}) async-start(f32[128,1,1152]{2,1,0:T(1,128)} %broadcast_in_dim.38), calls=%async_computation.1 | async-start | bytes 1179648 | tf_op jit(solution)/shard_map/all_to_all | solution.py:441
  133.6 0.6 copy-done.15
  134.2 0.6 copy-done.17
  134.9 20.8 %shard_map.208 = bf16[2,64,64,128]{3,2,1,0:T(8,128)(2,1)} custom-call(s32[2,8]{1,0:T(2,128)} %nb.11, s32[2]{0:T(128)} %ocean.5, bf16[2,64,64,128]{3,2,1,0:T(8,128)(2,1)} %get-tuple-element.33.above.below.g.grad, bf16[2,3,64,128]{3,2,1,0:T(8,128)(2,1)} %copy-done.5, bf16[2,3,64,128]{3,2,1,0:T(8,128)(2,1)} %copy-done.6, bf16[288,128]{1,0:T(8,128)(2,1)} %copy-done.15, ...), custom_call_target="tpu_custom_call" | custom-call | flops 10000000000 | bytes 10000000 | tf_op jit(solution)/shard_map/pallas_call | solution.py:49
  155.6 0.8 copy-done
  156.4 2.1 %shard_map.210 = (f32[7,7,128]{2,1,0:T(8,128)}, f32[1,128]{1,0:T(1,128)}, f32[1,128]{1,0:T(1,128)}, f32[1,128]{1,0:T(1,128)}, f32[128,512]{1,0:T(8,128)}, /*inde...) custom-call(f32[1152,128]{1,0:T(8,128)} %bitcast.31, f32[4,128]{1,0:T(4,128)} %pad_maximum_fusion.1.rows, ...), custom_call_target="tpu_custom_call" | custom-call | tf_op jit(solution)/shard_map/pallas_call | solution.py:49
  (48 shorter events, 1.7 us)
Async XLA Ops:
  0.6 10.4 %copy-start.1 = (bf16[128,512]{1,0:T(8,128)(2,1)S(1)}, bf16[128,512]{1,0:T(8,128)(2,1)}, u32[]{:S(2)}) copy-start(bf16[128,512]{1,0:T(8,128)(2,1)} %w_up.1) | copy-start | bytes 393220
  0.7 10.5 %copy-start.10 = (f32[128]{0:T(128)S(1)}, f32[128]{0:T(128)}, u32[]{:S(2)}) copy-start(f32[128]{0:T(128)} %param.20) | copy-start | bytes 1540
  0.7 10.7 %copy-start.2 = (bf16[512,128]{1,0:T(8,128)(2,1)S(1)}, bf16[512,128]{1,0:T(8,128)(2,1)}, u32[]{:S(2)}) copy-start(bf16[512,128]{1,0:T(8,128)(2,1)} %w_down.1) | copy-start | bytes 393220
  0.7 10.8 %copy-start.9 = (f32[128]{0:T(128)S(1)}, f32[128]{0:T(128)}, u32[]{:S(2)}) copy-start(f32[128]{0:T(128)} %param.25) | copy-start | bytes 1540
  0.7 11.5 %copy-start.8 = (f32[128]{0:T(128)S(1)}, f32[128]{0:T(128)}, u32[]{:S(2)}) copy-start(f32[128]{0:T(128)} %param.19) | copy-start | bytes 1540
  0.7 11.7 %copy-start.7 = (f32[7,7,128]{2,1,0:T(8,128)S(1)}, f32[7,7,128]{2,1,0:T(8,128)}, u32[]{:S(2)}) copy-start(f32[7,7,128]{2,1,0:T(8,128)} %param.17) | copy-start | bytes 75268
  0.7 12.5 %copy-start.11 = (f32[512]{0:T(512)S(1)}, f32[512]{0:T(512)}, u32[]{:S(2)}) copy-start(f32[512]{0:T(512)} %param.22) | copy-start | bytes 6148
  2.7 11.1 %collective-permute-start = (bf16[2,3,64,128]{3,2,1,0:T(8,128)(2,1)}, bf16[2,3,64,128]{3,2,1,0:T(8,128)(2,1)S(1)}, u32[]{:S(2)}, u32[]{:S(2)}) collective-permute-start(bf16[2,3,64,128]{3,2,1,0:T(8,128)(2,1)} %get-tuple-element.29), channel_id=1, source_target_pairs={{0,28},{4,24},{8,20},{12,16},{16,44},{20,40},{24,36},{28,32},{32,6... | collective-permute-start | bytes 294920 | tf_op jit(solution)/shard_map/ppermute | solution.py:127
  9.7 7.6 %collective-permute-start.1 = (bf16[2,3,64,128]{3,2,1,0:T(8,128)(2,1)}, bf16[2,3,64,128]{3,2,1,0:T(8,128)(2,1)S(1)}, u32[]{:S(2)}, u32[]{:S(2)}) collective-permute-start(bf16[2,3,64,128]{3,2,1,0:T(8,128)(2,1)} %get-tuple-element.30), channel_id=1, source_target_pairs={{28,0},{24,4},{20,8},{16,12},{44,16},{40,20},{36,24},{32,28},{60,3... | collective-permute-start | bytes 294920 | tf_op jit(solution)/shard_map/ppermute | solution.py:128
  13.8 3.5 %copy-start.3 = (bf16[2,3,64,128]{3,2,1,0:T(8,128)(2,1)}, bf16[2,3,64,128]{3,2,1,0:T(8,128)(2,1)S(1)}, u32[]{:S(2)}) copy-start(bf16[2,3,64,128]{3,2,1,0:T(8,128)(2,1)S(1)} %collective-permute-done.from_prev) | copy-start | bytes 294916
  17.3 0.6 copy-start.4
  19.7 5.2 %collective-permute-start.2 = (bf16[288,128]{1,0:T(8,128)(2,1)}, bf16[288,128]{1,0:T(8,128)(2,1)S(1)}, u32[]{:S(2)}, u32[]{:S(2)}) collective-permute-start(bf16[288,128]{1,0:T(8,128)(2,1)} %get-tuple-element.31), channel_id=1, source_target_pairs={{0,4},{4,8},{8,12},{16,20},{20,24},{24,28},{32,36},{36,40},{40,44}... | collective-permute-start | bytes 221192 | tf_op jit(solution)/shard_map/ppermute | solution.py:144
  21.6 5.9 %collective-permute-start.3 = (bf16[288,128]{1,0:T(8,128)(2,1)}, bf16[288,128]{1,0:T(8,128)(2,1)S(1)}, u32[]{:S(2)}, u32[]{:S(2)}) collective-permute-start(bf16[288,128]{1,0:T(8,128)(2,1)} %get-tuple-element.32), channel_id=1, source_target_pairs={{4,0},{8,4},{12,8},{20,16},{24,20},{28,24},{36,32},{40,36},{44,40}... | collective-permute-start | bytes 221192 | tf_op jit(solution)/shard_map/ppermute | solution.py:145
  24.9 3.3 %copy-start.16 = (bf16[288,128]{1,0:T(8,128)(2,1)}, bf16[288,128]{1,0:T(8,128)(2,1)S(1)}, u32[]{:S(2)}) copy-start(bf16[288,128]{1,0:T(8,128)(2,1)S(1)} %collective-permute-done.2.chain_prev) | copy-start | bytes 221188
  27.5 0.7 copy-start.18
  74.2 27.7 %copy-start.14 = (bf16[2,3,64,128]{3,2,1,0:T(8,128)(2,1)S(1)}, bf16[2,3,64,128]{3,2,1,0:T(8,128)(2,1)}, u32[]{:S(2)}) copy-start(bf16[2,3,64,128]{3,2,1,0:T(8,128)(2,1)} %get-tuple-element.34) | copy-start | bytes 294916
  74.2 33.1 %copy-start.13 = (bf16[2,3,64,128]{3,2,1,0:T(8,128)(2,1)S(1)}, bf16[2,3,64,128]{3,2,1,0:T(8,128)(2,1)}, u32[]{:S(2)}) copy-start(bf16[2,3,64,128]{3,2,1,0:T(8,128)(2,1)} %get-tuple-element.35) | copy-start | bytes 294916
  93.9 30.2 %all-to-all-start = ((f32[128,1,1152]{2,1,0:T(1,128)}), f32[128,1,1152]{2,1,0:T(1,128)S(1)}, u32[]{:S(2)}, u32[]{:S(2)}) async-start(f32[128,1,1152]{2,1,0:T(1,128)} %bitcast.33), calls=%async_computation | async-start | bytes 1179648 | tf_op jit(solution)/shard_map/all_to_all | solution.py:438
  101.9 13.1 %collective-permute-start.4 = (bf16[2,3,64,128]{3,2,1,0:T(8,128)(2,1)S(1)}, bf16[2,3,64,128]{3,2,1,0:T(8,128)(2,1)S(1)}, u32[]{:S(2)}, u32[]{:S(2)}) collective-permute-start(bf16[2,3,64,128]{3,2,1,0:T(8,128)(2,1)S(1)} %copy-done.14), channel_id=1, source_target_pairs={{0,28},{4,24},{8,20},{12,16},{16,44},{20,40},{24,36},{28,32},{32,6... | collective-permute-start | bytes 294920 | tf_op jit(solution)/shard_map/ppermute | solution.py:127
  107.3 16.3 %copy-start.12 = (f32[128]{0:T(128)S(1)}, f32[128]{0:T(128)}, u32[]{:S(2)}) copy-start(f32[128]{0:T(128)} %param.24) | copy-start | bytes 1540
  107.3 9.5 %collective-permute-start.5 = (bf16[2,3,64,128]{3,2,1,0:T(8,128)(2,1)S(1)}, bf16[2,3,64,128]{3,2,1,0:T(8,128)(2,1)S(1)}, u32[]{:S(2)}, u32[]{:S(2)}) collective-permute-start(bf16[2,3,64,128]{3,2,1,0:T(8,128)(2,1)S(1)} %copy-done.13), channel_id=1, source_target_pairs={{28,0},{24,4},{20,8},{16,12},{44,16},{40,20},{36,24},{32,28},{60,3... | collective-permute-start | bytes 294920 | tf_op jit(solution)/shard_map/ppermute | solution.py:128
  115.0 1.9 %copy-start.5 = (bf16[2,3,64,128]{3,2,1,0:T(8,128)(2,1)}, bf16[2,3,64,128]{3,2,1,0:T(8,128)(2,1)S(1)}, u32[]{:S(2)}) copy-start(bf16[2,3,64,128]{3,2,1,0:T(8,128)(2,1)S(1)} %collective-permute-done.4.from_prev) | copy-start | bytes 294916
  116.8 0.6 copy-start.6
  119.2 14.4 %collective-permute-start.6 = (bf16[288,128]{1,0:T(8,128)(2,1)}, bf16[288,128]{1,0:T(8,128)(2,1)S(1)}, u32[]{:S(2)}, u32[]{:S(2)}) collective-permute-start(bf16[288,128]{1,0:T(8,128)(2,1)} %get-tuple-element.36), channel_id=1, source_target_pairs={{0,4},{4,8},{8,12},{16,20},{20,24},{24,28},{32,36},{36,40},{40,44}... | collective-permute-start | bytes 221192 | tf_op jit(solution)/shard_map/ppermute | solution.py:144
  121.2 12.5 %collective-permute-start.7 = (bf16[288,128]{1,0:T(8,128)(2,1)}, bf16[288,128]{1,0:T(8,128)(2,1)S(1)}, u32[]{:S(2)}, u32[]{:S(2)}) collective-permute-start(bf16[288,128]{1,0:T(8,128)(2,1)} %get-tuple-element.37), channel_id=1, source_target_pairs={{4,0},{8,4},{12,8},{20,16},{24,20},{28,24},{36,32},{40,36},{44,40}... | collective-permute-start | bytes 221192 | tf_op jit(solution)/shard_map/ppermute | solution.py:145
  125.7 29.9 %all-to-all-start.1 = ((f32[128,1,1152]{2,1,0:T(1,128)}), f32[128,1,1152]{2,1,0:T(1,128)S(1)}, u32[]{:S(2)}, u32[]{:S(2)}) async-start(f32[128,1,1152]{2,1,0:T(1,128)} %broadcast_in_dim.38), calls=%async_computation.1 | async-start | bytes 1179648 | tf_op jit(solution)/shard_map/all_to_all | solution.py:441
  133.6 0.6 copy-start.15
  134.2 0.6 copy-start.17
  155.6 0.8 copy-start
